TPU v7x, 256 devices: a whole 4x4x8 slice. The times are simulated.
256 devices in a mesh: ctx: 32 (over y, z), mp: 8 (over x, core).
Axes of the slice: x: 4, y: 4, z: 8, core: 2. Of those that a mesh axis runs over, the one named last changes fastest.
Arguments:
- tokens: bfloat16 [32768, 4096], P('ctx'), may hold values from -6 to 6
- lru_in_weight: bfloat16 [4096, 4096], P(None, 'mp'), may hold values from -0.09375 to 0.09375
- gelu_weight: bfloat16 [4096, 4096], P(None, 'mp'), may hold values from -0.09375 to 0.09375
- conv_weight: bfloat16 [4, 4096], P(None, 'mp'), may hold values from -3 to 3
- recur_gate_weight: bfloat16 [16, 256, 256], P('mp'), may hold values from -0.375 to 0.375
- input_gate_weight: bfloat16 [16, 256, 256], P('mp'), may hold values from -0.375 to 0.375
- decay_rate: float32 [4096], P('mp'), may hold values from 6.1035155e-07 to 0.02
- segment_pos: int32 [32768], P('ctx'), may hold values from 0 to 16895, as said below
- source_row: int32 [32768], P('ctx'), may hold values from 0 to 32767, as said below
Outputs:
- block_out: bfloat16 [32768, 4096], P(('ctx', 'mp'))
Inputs may be any that keep to these rules, and one draw needn't show every extreme that they name: `source_row`: window position p belongs to context shard c = p // 1024. Every loader row appears once. Loader shard l sends to context shard c exactly the rows l * 1024 + c * 32 to l * 1024 + (c + 1) * 32 - 1. `segment_pos`: counts positions since the last document start; it rises by one except at document starts, where it is 0. The first document covers rows 0 to 16895; the other 7 documents start at row 16896 and at 6 further rows after it.
All inputs are finite; a program needn't handle non-finite values.
Results may differ from a plain program's by a relative error of at most 0.012.
Values may be sent and summed in bfloat16 or wider, within the bound.
A program may use at most 128 MiB of HBM per device.

v0:
```python
import jax
import jax.numpy as jnp
from jax import lax
from jax.sharding import PartitionSpec as P


def shifted(value, axis, steps):
    count = lax.axis_size(axis)
    initial, last = (max(0, -steps), min(count, count - steps))
    return lax.ppermute(value, axis, [(source, source + steps) for source in range(initial, last)])


def copy_for_each(array, axis):
    copies = jnp.broadcast_to(array, (lax.axis_size(axis), *array.shape))
    return lax.all_to_all(copies, axis, split_axis=0, concat_axis=0, tiled=True)


def gathered_once(array, axis):
    leaves = jax.tree.leaves(array)
    turns = sorted(range(len(leaves)), key=lambda k: -leaves[k].size)
    width = (1, *leaves[turns[0]].shape)[-1]
    lines = [
        jnp.pad(leaves[k].reshape(-1), (0, -leaves[k].size % width)).reshape(-1, width)
        for k in turns
    ]
    both, at, found = (copy_for_each(jnp.concatenate(lines), axis), 0, {})
    for k, line in zip(turns, lines):
        slab = both[:, at : at + len(line)].reshape(len(both), -1)
        found[k] = slab[:, : leaves[k].size].reshape(-1, *leaves[k].shape)
        at += len(line)
    numbers = iter(range(len(leaves)))
    return jax.tree.map(lambda _: found[next(numbers)], array)


def joined_by_halves(pieces, combine):
    while len(jax.tree.leaves(pieces)[0]) > 1:
        pieces = jax.vmap(combine)(
            *(jax.tree.map(lambda part: part[side::2], pieces) for side in (0, 1))
        )
    return jax.tree.map(lambda part: part[0], pieces)


def entering(array, axis, combine, identity):
    peers, position = (lax.axis_size(axis), lax.axis_index(axis))
    passed = jnp.arange(peers) < position

    def kept(part, zero, own):
        part = jnp.where(
            passed.reshape(-1, *(1 for _ in own.shape)), part, jnp.asarray(zero, own.dtype)
        )
        return part

    pieces = gathered_once(array, axis)
    return joined_by_halves(jax.tree.map(kept, pieces, identity, array), combine)


def affine_join(earlier, later):
    return (earlier[0] * later[0], later[0] * earlier[1] + later[1])


def project_rows(rows_in, lru_in_weight, gelu_weight):
    branch = jnp.dot(rows_in, lru_in_weight, preferred_element_type=jnp.float32).astype(
        jnp.bfloat16
    )
    gate_rows = jnp.dot(rows_in, gelu_weight, preferred_element_type=jnp.float32).astype(
        jnp.bfloat16
    )
    return (branch, gate_rows)


def block_gate(grouped, weights, tok_rows, width_local):
    mixed = jnp.einsum("tkb,kbc->tkc", grouped, weights, preferred_element_type=jnp.float32)
    return jax.nn.sigmoid(mixed.reshape(tok_rows, width_local))


def gated_rows(state_rows, gate_rows):
    return (
        state_rows.astype(jnp.float32)
        * jax.nn.gelu(gate_rows.astype(jnp.float32), approximate=True)
    ).astype(jnp.bfloat16)


def body(
    tokens,
    lru_in_weight,
    gelu_weight,
    conv_weight,
    recur_gate_weight,
    input_gate_weight,
    decay_rate,
    segment_pos,
    source_row,
):
    tok_rows = tokens.shape[0]
    share_rows = tok_rows // lax.axis_size("ctx")
    here_index = lax.axis_index("ctx")
    recv_index = (
        source_row // tok_rows * share_rows + source_row % tok_rows - here_index * share_rows
    )
    branch_loader, gate_loader = project_rows(tokens, lru_in_weight, gelu_weight)
    branch_moved = lax.all_to_all(branch_loader, "ctx", split_axis=0, concat_axis=0, tiled=True)
    branch = jnp.take(branch_moved, recv_index, axis=0)
    width_local = branch.shape[1]
    tap_count = conv_weight.shape[0]
    rim_rows = shifted(branch[tok_rows - (tap_count - 1) :], "ctx", 1)
    extended = jnp.concatenate([rim_rows, branch], axis=0).astype(jnp.float32)
    conv_sum = jnp.zeros((tok_rows, width_local), jnp.float32)
    for offset in range(tap_count):
        live_mask = (segment_pos >= offset).astype(jnp.float32)[:, None]
        lower = tap_count - 1 - offset
        conv_sum = (
            conv_sum
            + conv_weight[offset].astype(jnp.float32)[None, :]
            * extended[lower : lower + tok_rows]
            * live_mask
        )
    conv_out = conv_sum.astype(jnp.bfloat16)
    blocks = recur_gate_weight.shape[0]
    block_size = recur_gate_weight.shape[1]
    grouped = conv_out.reshape(tok_rows, blocks, block_size)
    recur_gate = block_gate(grouped, recur_gate_weight, tok_rows, width_local)
    input_gate = block_gate(grouped, input_gate_weight, tok_rows, width_local)
    log_decay = -8.0 * recur_gate * decay_rate[None, :]
    decay_step = jnp.exp(log_decay)
    starts = (segment_pos == 0)[:, None]
    scale_in = jnp.where(starts, jnp.float32(1.0), jnp.sqrt(-jnp.expm1(2.0 * log_decay)))
    drive_term = scale_in * input_gate * conv_out.astype(jnp.float32)
    carried = jnp.where(starts, jnp.float32(0.0), decay_step)
    cum_decay, local_state = lax.associative_scan(affine_join, (carried, drive_term), axis=0)
    summary = (cum_decay[tok_rows - 1], local_state[tok_rows - 1])
    identity = (jnp.ones_like(summary[0]), jnp.zeros_like(summary[1]))
    incoming = entering(summary, "ctx", affine_join, identity)[1]
    full_state = local_state + cum_decay * incoming[None, :]
    state_rows = full_state.astype(jnp.bfloat16)
    state_loader = jnp.zeros_like(state_rows).at[recv_index].set(state_rows)
    state_home = lax.all_to_all(state_loader, "ctx", split_axis=0, concat_axis=0, tiled=True)
    home_out = gated_rows(state_home, gate_loader)
    return lax.all_to_all(home_out, "mp", split_axis=0, concat_axis=1, tiled=True)


def solution(mesh):
    in_specs = (
        P("ctx", None),
        P(None, "mp"),
        P(None, "mp"),
        P(None, "mp"),
        P("mp", None, None),
        P("mp", None, None),
        P("mp"),
        P("ctx"),
        P("ctx"),
    )
    out_specs = P(("ctx", "mp"), None)
    return jax.shard_map(body, mesh=mesh, in_specs=in_specs, out_specs=out_specs, check_vma=False)
```

profile of v0, /device:TPU:1, one launch (start us, length us, event | category | flops | bytes accessed | tf_op | source)
XLA Modules:
  0.0 247.7 jit_solution(7344321183128220661)
XLA Ops:
  0.0 10.1 %convolution_convert_fusion.1 = bf16[1024,512]{1,0:T(8,128)(2,1)} fusion(bf16[1024,4096]{1,0:T(8,128)(2,1)} %param.9, bf16[4096,512]{1,0:T(8,128)(2,1)} %param.10), kind=kOutput, calls=%fused_computation.31 | convolution fusion | flops 4295491584 | bytes 13631488 | tf_op jit(solution)/shard_map/dot_general | solution.py:62
  10.1 12.2 %all-to-all-start = ((bf16[32,32,512]{2,1,0:T(8,128)(2,1)}), bf16[32,32,512]{2,1,0:T(8,128)(2,1)S(1)}, u32[]{:S(2)}, u32[]{:S(2)}) async-start(bf16[32,32,512]{2,1,0:T(8,128)(2,1)} %bitcast.1), calls=%async_computation | async-start | bytes 2097152 | tf_op jit(solution)/shard_map/all_to_all | solution.py:101
  22.3 24.8 %all-to-all-done = bf16[32,32,512]{2,1,0:T(8,128)(2,1)S(1)} async-done(((bf16[32,32,512]{2,1,0:T(8,128)(2,1)}), bf16[32,32,512]{2,1,0:T(8,128)(2,1)S(1)}, u32[]{:S(2)}, u32[]{:S(2)}) %all-to-all-start) | async-done | bytes 1048608 | tf_op jit(solution)/shard_map/all_to_all | solution.py:101
  47.1 4.0 %gather_fusion = bf16[1024,512]{1,0:T(8,128)(2,1)S(1)} fusion(bf16[1024,512]{1,0:T(8,128)(2,1)S(1)} %bitcast.39, s32[1024]{0:T(1024)S(1)} %broadcast_clamp_fusion), kind=kCustom, calls=%fused_computation | custom fusion | bytes 2101248 | tf_op jit(solution)/shard_map/jit(_take)/gather | solution.py:102
  51.1 0.2 broadcast_select_fusion
  51.3 5.7 %collective-permute-start = (bf16[3,512]{1,0:T(4,128)(2,1)S(1)}, bf16[3,512]{1,0:T(4,128)(2,1)S(1)}, u32[]{:S(2)}, u32[]{:S(2)}) collective-permute-start(bf16[3,512]{1,0:T(4,128)(2,1)S(1)} %slice.517), channel_id=1, source_target_pairs={{0,8},{8,16},{16,24},{24,32},{32,40},{40,48},{48,56},{56,64},{64,7... | collective-permute-start | bytes 9224 | tf_op jit(solution)/shard_map/ppermute | solution.py:10
  57.0 0.5 collective-permute-done
  57.6 0.3 maximum_convert_fusion
  57.9 1.5 fusion.9
  59.4 2.1 add_divide_fusion
  61.5 3.0 %copy.22 = f32[1024,512]{1,0:T(8,128)} copy(f32[1024,512]{0,1:T(8,128)} %bitcast.43) | data formatting | bytes 4194304 | tf_op jit(solution)/shard_map/div | solution.py:73
  64.5 2.1 add_divide_fusion.1
  66.6 2.9 %copy.19 = f32[1024,512]{1,0:T(8,128)} copy(f32[1024,512]{0,1:T(8,128)} %bitcast.42) | data formatting | bytes 4194304 | tf_op jit(solution)/shard_map/div | solution.py:73
  69.5 5.8 %convert_multiply_fusion.3 = (f32[1024,512]{1,0:T(8,128)S(1)}, f32[1024,512]{1,0:T(8,128)}) fusion(f32[1024,512]{1,0:T(8,128)} %copy.22, f32[1024,512]{1,0:T(8,128)} %copy.19, f32[512]{0:T(512)S(1)} %broadcast_multiply_fusion, pred[1024]{0:T(1024)(128)(4,1)S(1)} %get-tuple-element.59, f32[1024]{0:T(1024)S(1)} %get-tuple-element.62, ...), kind=kLoop, calls=%fused_computation.27 | loop fusion | flops 10485760 | bytes 16804864 | tf_op jit(solution)/shard_map/mul | solution.py:127
  75.3 1.3 copy-done.3
  76.6 6.3 %slice.472 = f32[511,512]{1,0:T(8,128)} slice(f32[1024,512]{1,0:T(8,128)} %copy-done.3), slice={[2:1024:2], [0:512:1]} | slice | bytes 2093056 | tf_op jit(solution)/shard_map/slice | solution.py:129
  82.9 5.2 %slice.402 = f32[512,512]{1,0:T(8,128)S(1)} slice(f32[1024,512]{1,0:T(8,128)} %copy-done.3), slice={[1:1024:2], [0:512:1]} | slice | bytes 2097152 | tf_op jit(solution)/shard_map/slice | solution.py:129
  88.2 6.3 %slice.401 = f32[512,512]{1,0:T(8,128)} slice(f32[1024,512]{1,0:T(8,128)} %copy-done.3), slice={[0:1023:2], [0:512:1]} | slice | bytes 2097152 | tf_op jit(solution)/shard_map/slice | solution.py:129
  94.4 3.5 %slice.404 = f32[512,512]{1,0:T(8,128)} slice(f32[1024,512]{1,0:T(8,128)S(1)} %copy-done.2), slice={[0:1023:2], [0:512:1]} | slice | bytes 2097152 | tf_op jit(solution)/shard_map/slice | solution.py:129
  97.9 3.5 %slice.400 = f32[512,512]{1,0:T(8,128)} slice(f32[1024,512]{1,0:T(8,128)S(1)} %copy-done.2), slice={[1:1024:2], [0:512:1]} | slice | bytes 2097152 | tf_op jit(solution)/shard_map/slice | solution.py:129
  101.4 3.6 %slice.399 = f32[511,512]{1,0:T(8,128)} slice(f32[1024,512]{1,0:T(8,128)S(1)} %copy-done.2), slice={[2:1024:2], [0:512:1]} | slice | bytes 2093056 | tf_op jit(solution)/shard_map/slice | solution.py:129
  105.0 2.3 multiply_add_fusion
  107.3 2.1 slice.470
  109.4 0.5 slice.408
  110.0 0.5 slice.407
  110.5 0.5 slice.410
  111.1 0.5 slice.406
  111.6 2.1 slice.405
  113.8 0.2 multiply_add_fusion.1
  114.0 0.3 slice.468
  114.3 0.3 slice.414
  114.7 0.3 slice.413
  115.0 0.3 slice.416
  115.3 0.3 slice.412
  115.7 0.3 slice.411
  119.0 0.8 add.307
  120.3 0.6 copy-done.11
  121.0 0.9 add.308
  121.9 0.9 add.296
  122.8 1.2 fusion.22
  124.1 0.8 copy-done.10
  125.2 2.1 pad.139
  127.3 4.7 %pad.159 = f32[512,512]{1,0:T(8,128)} pad(f32[256,512]{1,0:T(8,128)} %add.308, f32[]{:T(128)} %constant.73.clone.1), padding=1_0_1x0_0_0 | pad | bytes 1572868 | tf_op jit(solution)/shard_map/pad | solution.py:129
  131.9 2.4 add.309
  134.4 1.2 add.298
  135.6 0.2 copy-done.4
  135.8 0.5 copy-done.6
  136.3 0.3 copy-done.7
  136.6 1.7 fusion.18
  138.4 0.3 pad.160
  138.7 1.3 pad_maximum_fusion
  140.1 4.9 %pad.140 = f32[1024,512]{1,0:T(8,128)} pad(f32[512,512]{1,0:T(8,128)S(1)} %pad_maximum_fusion, f32[]{:T(128)} %constant.73.clone.1), padding=0_1_1x0_0_0 | pad | bytes 3145732 | tf_op jit(solution)/shard_map/pad | solution.py:129
  145.0 8.6 %pad.141 = f32[1024,512]{1,0:T(8,128)} pad(f32[512,512]{1,0:T(8,128)} %add.298, f32[]{:T(128)} %constant.73.clone.1), padding=1_0_1x0_0_0 | pad | bytes 3145732 | tf_op jit(solution)/shard_map/pad | solution.py:129
  153.6 4.9 %pad.161 = f32[1024,512]{1,0:T(8,128)} pad(f32[512,512]{1,0:T(8,128)S(1)} %copy-done.5, f32[]{:T(128)} %constant.73.clone.1), padding=1_0_1x0_0_0 | pad | bytes 3145732 | tf_op jit(solution)/shard_map/pad | solution.py:129
  158.4 0.7 slice_add_fusion.1
  159.2 0.7 slice_add_fusion.2
  159.9 0.7 broadcast_in_dim.81
  160.6 7.6 %all-to-all-start.1 = ((f32[32,2,512]{2,1,0:T(2,128)}), f32[32,2,512]{2,1,0:T(2,128)S(1)}, u32[]{:S(2)}, u32[]{:S(2)}) async-start(f32[32,2,512]{2,1,0:T(2,128)} %broadcast_in_dim.81), calls=%async_computation.1 | async-start | bytes 262144 | tf_op jit(solution)/shard_map/all_to_all | solution.py:15
  168.2 9.1 %all-to-all-done.1 = f32[32,2,512]{2,1,0:T(2,128)S(1)} async-done(((f32[32,2,512]{2,1,0:T(2,128)}), f32[32,2,512]{2,1,0:T(2,128)S(1)}, u32[]{:S(2)}, u32[]{:S(2)}) %all-to-all-start.1) | async-done | bytes 131104 | tf_op jit(solution)/shard_map/all_to_all | solution.py:15
  178.0 6.7 %scatter_custom_fusion = bf16[1024,512]{1,0:T(8,128)(2,1)S(1)} fusion(s32[1024]{0:T(1024)S(1)} %get-tuple-element.6, f32[1024,512]{1,0:T(8,128)S(1)} %pad.160, f32[1024,512]{1,0:T(8,128)} %pad.161, f32[1024,512]{1,0:T(8,128)} %pad.140, f32[1024,512]{1,0:T(8,128)} %pad.141, f32[512]{0:T(512)S(1)} %bitcast.56, bf16[]{:T(256)} %constant.26.clone.1), kind=kCustom, calls=%fused_computation.33 | custom fusion | flops 2621440 | bytes 9439234 | tf_op jit(solution)/shard_map/scatter | solution.py:135
  184.7 25.2 %all_to_all.45 = bf16[32,32,512]{2,1,0:T(8,128)(2,1)S(1)} all-to-all(bf16[32,32,512]{2,1,0:T(8,128)(2,1)S(1)} %bitcast.41), channel_id=1, replica_groups=mesh['ctx'=32,'mp'=8] {'ctx'}, dimensions={0} | all-to-all | bytes 2097152 | tf_op jit(solution)/shard_map/all_to_all | solution.py:136
  209.9 9.6 %fusion.6 = bf16[1024,512]{1,0:T(8,128)(2,1)S(1)} fusion(bf16[1024,512]{1,0:T(8,128)(2,1)S(1)} %bitcast.44, bf16[1024,4096]{1,0:T(8,128)(2,1)} %param.9, bf16[4096,512]{1,0:T(8,128)(2,1)} %param.11), kind=kOutput, calls=%fused_computation.12 | convolution fusion | flops 4301783040 | bytes 14680064 | tf_op jit(solution)/shard_map/dot_general | solution.py:65
  219.5 27.1 %all_to_all.46 = bf16[8,128,512]{2,1,0:T(8,128)(2,1)S(1)} all-to-all(bf16[8,128,512]{2,1,0:T(8,128)(2,1)S(1)} %bitcast.45), channel_id=1, replica_groups=mesh['ctx'=32,'mp'=8] {'mp'}, dimensions={0} | all-to-all | bytes 2097152 | tf_op jit(solution)/shard_map/all_to_all | solution.py:138
  246.6 1.1 copy.30
  (182 shorter events, 4.2 us)
Async XLA Ops:
  0.0 59.4 %copy-start = (bf16[2,256,256]{2,1,0:T(8,128)(2,1)S(1)}, bf16[2,256,256]{2,1,0:T(8,128)(2,1)}, u32[]{:S(2)}) copy-start(bf16[2,256,256]{2,1,0:T(8,128)(2,1)} %param.14) | copy-start | bytes 786436
  10.1 12.2 %copy-start.13 = (s32[1024]{0:T(1024)S(1)}, s32[1024]{0:T(1024)}, u32[]{:S(2)}) copy-start(s32[1024]{0:T(1024)} %param.17) | copy-start | bytes 12292
  10.1 12.2 %copy-start.12 = (bf16[4,512]{1,0:T(4,128)(2,1)S(1)}, bf16[4,512]{1,0:T(4,128)(2,1)}, u32[]{:S(2)}) copy-start(bf16[4,512]{1,0:T(4,128)(2,1)} %param.12) | copy-start | bytes 12292
  10.1 12.3 %copy-start.14 = (s32[1024]{0:T(1024)S(1)}, s32[1024]{0:T(1024)}, u32[]{:S(2)}) copy-start(s32[1024]{0:T(1024)} %param.16) | copy-start | bytes 12292
  10.1 37.0 %all-to-all-start = ((bf16[32,32,512]{2,1,0:T(8,128)(2,1)}), bf16[32,32,512]{2,1,0:T(8,128)(2,1)S(1)}, u32[]{:S(2)}, u32[]{:S(2)}) async-start(bf16[32,32,512]{2,1,0:T(8,128)(2,1)} %bitcast.1), calls=%async_computation | async-start | bytes 2097152 | tf_op jit(solution)/shard_map/all_to_all | solution.py:101
  51.1 5.9 %copy-start.15 = (f32[512]{0:T(512)S(1)}, f32[512]{0:T(512)}, u32[]{:S(2)}) copy-start(f32[512]{0:T(512)} %param.15) | copy-start | bytes 6148
  51.3 6.2 %collective-permute-start = (bf16[3,512]{1,0:T(4,128)(2,1)S(1)}, bf16[3,512]{1,0:T(4,128)(2,1)S(1)}, u32[]{:S(2)}, u32[]{:S(2)}) collective-permute-start(bf16[3,512]{1,0:T(4,128)(2,1)S(1)} %slice.517), channel_id=1, source_target_pairs={{0,8},{8,16},{16,24},{24,32},{32,40},{40,48},{48,56},{56,64},{64,7... | collective-permute-start | bytes 9224 | tf_op jit(solution)/shard_map/ppermute | solution.py:10
  61.5 3.0 %copy-start.16 = (bf16[2,256,256]{2,1,0:T(8,128)(2,1)S(1)}, bf16[2,256,256]{2,1,0:T(8,128)(2,1)}, u32[]{:S(2)}) copy-start(bf16[2,256,256]{2,1,0:T(8,128)(2,1)} %param.13) | copy-start | bytes 786436
  75.3 1.3 copy-start.3
  82.9 11.5 %copy-start.2 = (f32[1024,512]{1,0:T(8,128)S(1)}, f32[1024,512]{1,0:T(8,128)}, u32[]{:S(2)}) copy-start(f32[1024,512]{1,0:T(8,128)} %get-tuple-element.8) | copy-start | bytes 6291460
  120.0 1.0 copy-start.11
  120.9 1.8 copy-start.8
  120.9 1.8 copy-start.9
  123.9 1.0 copy-start.10
  134.4 1.4 copy-start.4
  134.4 1.9 copy-start.6
  134.4 2.2 copy-start.7
  145.0 8.6 %copy-start.5 = (f32[512,512]{1,0:T(8,128)S(1)}, f32[512,512]{1,0:T(8,128)}, u32[]{:S(2)}) copy-start(f32[512,512]{1,0:T(8,128)} %add.309) | copy-start | bytes 3145732
  160.6 16.7 %all-to-all-start.1 = ((f32[32,2,512]{2,1,0:T(2,128)}), f32[32,2,512]{2,1,0:T(2,128)S(1)}, u32[]{:S(2)}, u32[]{:S(2)}) async-start(f32[32,2,512]{2,1,0:T(2,128)} %broadcast_in_dim.81), calls=%async_computation.1 | async-start | bytes 262144 | tf_op jit(solution)/shard_map/all_to_all | solution.py:15
  219.5 28.2 %copy-start.1 = (bf16[2,256,256]{2,1,0:T(8,128)(2,1)S(1)}, bf16[2,256,256]{2,1,0:T(8,128)(2,1)}, u32[]{:S(2)}) copy-start(bf16[2,256,256]{2,1,0:T(8,128)(2,1)} %param.14) | copy-start | bytes 786436
where the time goes:
time: 249 us; the launch traced here: 248 us
  local copies, waits for them, and re-layouts  80.4 us (32%)
  blocking collectives  52.4 us (21%)
  waiting for transfers between devices  34.4 us (14%)
  other arithmetic  30.2 us (12%)
  starting transfers between devices  25.4 us (10%)
  matrix products  23.9 us (10%)
    slice x68, local copies, waits for them, and re-layouts, body(): lax.associative_scan(affine_join, (carried, drive_term), axis=0)  38.2 us
    all_to_all x1, blocking collectives, body(): lax.all_to_all(home_out, 'mp', split_axis=0, concat_axis=1, tiled=True)  27.1 us
    pad x36, local copies, waits for them, and re-layouts, body(): lax.associative_scan(affine_join, (carried, drive_term), axis=0)  26.4 us
    all_to_all x1, blocking collectives, body(): lax.all_to_all(state_loader, 'ctx', split_axis=0, concat_axis=0, tiled=True)  25.2 us
    all_to_all x1, waiting for transfers between devices, body(): lax.all_to_all(branch_loader, 'ctx', split_axis=0, concat_axis=0, tiled=T...  24.8 us
    all_to_all x1, starting transfers between devices, body(): lax.all_to_all(branch_loader, 'ctx', split_axis=0, concat_axis=0, tiled=T...  12.2 us
    dot_general x1, matrix products, project_rows(): jnp.dot(rows_in, lru_in_weight, preferred_element_type=jnp.float32)  10.1 us
    dot_general x1, matrix products, project_rows(): jnp.dot(rows_in, gelu_weight, preferred_element_type=jnp.float32)  9.59 us
  transfers between devices with their start and end apart: 3, of which 3 were waited for; matrix products, arithmetic and copies ran while one was open for 0% of the time, Pallas kernels for 0%

commit v1 on v0

v1 whole, which is shorter than its diff:
```python
import functools

import jax
import jax.numpy as jnp
from jax import lax
from jax.experimental import pallas as pl
from jax.experimental.pallas import tpu as pltpu
from jax.sharding import PartitionSpec as P

MESH = pl.DeviceIdType.MESH
ANY = pl.BlockSpec(memory_space=pl.ANY)
VMEM = pl.BlockSpec(memory_space=pltpu.VMEM)
BF = jnp.bfloat16
F32 = jnp.float32
SUB = 8
HEAD = 16
DOT = functools.partial(jnp.dot, preferred_element_type=F32)


def one_minus_exp_minus(v):
    poly = F32(1.0 / 40320.0)
    for order in (5040.0, 720.0, 120.0, 24.0, 6.0, 2.0, 1.0):
        poly = F32(1.0 / order) - v * poly
    return v * poly


def kernel(
    dims,
    tok_hbm,
    lru_hbm,
    gelu_hbm,
    conv_ref,
    recur_hbm,
    input_hbm,
    rate_ref,
    seg_ref,
    src_ref,
    out_hbm,
    tok,
    lru,
    gel,
    recw,
    inpw,
    seg_b,
    idx_b,
    perm,
    perm_t,
    send1,
    recv1,
    send2,
    recv2,
    gate,
    fin,
    orecv,
    win,
    conv,
    lin_r,
    lin_i,
    decay,
    state,
    ends,
    rim_s,
    rim_r,
    sum_s,
    sum_r,
    rows16,
    load_sem,
    out_sem,
    s1,
    r1,
    s2,
    r2,
    sm,
    rm,
    ss,
    rs,
    sr,
    rr,
):
    ny, nz, n_mp, blocks, bs = dims
    n_ctx = ny * nz
    rows_all, depth = tok.shape
    share = rows_all // n_ctx
    part = rows_all // ny
    seg_rows = rows_all // SUB
    mp_rows = rows_all // n_mp
    per_y = n_mp // ny
    c = lax.axis_index("ctx")
    m = lax.axis_index("mp")
    y, z, x = c // nz, lax.rem(c, nz), m // 2
    barrier = pltpu.get_barrier_semaphore()

    @pl.loop(1, n_ctx)
    def _(k):
        pl.semaphore_signal(
            barrier, inc=1, device_id={"ctx": lax.rem(c + k, n_ctx)}, device_id_type=MESH
        )

    @pl.loop(1, n_mp)
    def _(k):
        pl.semaphore_signal(
            barrier, inc=1, device_id={"mp": lax.rem(m + k, n_mp)}, device_id_type=MESH
        )

    def remote(src, dst, send_sem, recv_sem, **device):
        return pltpu.make_async_remote_copy(
            src_ref=src,
            dst_ref=dst,
            send_sem=send_sem,
            recv_sem=recv_sem,
            device_id=device,
            device_id_type=MESH,
        )

    def part_rows(k):
        return pl.ds(pl.multiple_of(lax.rem(y + k, ny) * part, part), part)

    def load_tok(k):
        return pltpu.make_async_copy(
            tok_hbm.at[part_rows(k)], tok.at[part_rows(k)], load_sem.at[k]
        )

    def load_w(hbm, buf, b, at):
        return pltpu.make_async_copy(
            hbm.at[:, b * bs : (b + 1) * bs], buf.at[b], load_sem.at[at]
        )

    at = ny
    lru_loads = [load_w(lru_hbm, lru, b, at + b) for b in range(blocks)]
    at += blocks
    gel_loads = [load_w(gelu_hbm, gel, b, at + b) for b in range(blocks)]
    at += blocks
    gate_loads = [
        pltpu.make_async_copy(recur_hbm, recw, load_sem.at[at]),
        pltpu.make_async_copy(input_hbm, inpw, load_sem.at[at + 1]),
    ]
    lru_loads[0].start()
    for k in range(ny):
        load_tok(k).start()
    for copy in lru_loads[1:] + gate_loads + gel_loads:
        copy.start()

    src = src_ref[...]
    idx = (src // rows_all) * share + lax.rem(src, rows_all) - c * share
    seg = seg_ref[...]
    for j in range(seg_rows):
        idx_b[j] = jnp.broadcast_to(idx[:, j : j + 1], (SUB, 128))
        seg_b[j] = jnp.broadcast_to(seg[:, j : j + 1], (SUB, 128))
    lanes = lax.broadcasted_iota(jnp.int32, (128, 128), 1)

    @pl.loop(0, rows_all // 128)
    def _(g):
        want = idx_b[pl.ds(g * 16, 16)].reshape(128, 128)
        here = pl.ds(pl.multiple_of(g * 128, 128), 128)
        for t in range(rows_all // 128):
            hot = jnp.where(want == lanes + t * 128, F32(1.0), F32(0.0))
            perm[here, t * 128 : (t + 1) * 128] = hot.astype(BF)
            perm_t[t * 128 : (t + 1) * 128, here] = hot.T.astype(BF)

    def project(b, k):
        rows = part_rows(k)
        branch = DOT(tok[rows, :], lru[b]).astype(BF)
        first = lax.rem(y + k, ny) * nz
        send1[b, pl.ds(first, nz)] = branch.reshape(nz, share, bs)

    def send_part(buf, into, b, k, s_sem, r_sem):
        first = lax.rem(y + k, ny) * nz
        for dz in range(nz):
            d = first + lax.rem(z + dz, nz)

            @pl.when(d != c)
            def _():
                remote(buf.at[b, d], into.at[b, c], s_sem.at[b, d], r_sem.at[b, c], ctx=d).start()

            @pl.when(d == c)
            def _():
                into[b, c] = buf[b, c]

    def gate_part(b, k):
        rows = part_rows(k)
        line = DOT(tok[rows, :], gel[b]).astype(BF).astype(F32)
        gate[b, rows, :] = jax.nn.gelu(line, approximate=True)

    lru_loads[0].wait()
    load_tok(0).wait()
    project(0, 0)
    pl.semaphore_wait(barrier, n_ctx + n_mp - 2)
    send_part(send1, recv1, 0, 0, s1, r1)

    @pl.loop(1, ny)
    def _(k):
        load_tok(k).wait()
        project(0, k)
        send_part(send1, recv1, 0, k, s1, r1)

    for b in range(1, blocks):
        lru_loads[b].wait()

        @pl.loop(0, ny)
        def _(k):
            project(b, k)
            send_part(send1, recv1, b, k, s1, r1)

    for copy in gate_loads + gel_loads:
        copy.wait()

    @pl.loop(0, ny)
    def _(k):
        gate_part(0, k)

    def wait_from(buf, b, sem, other_sem, source):
        @pl.when(source != c)
        def _():
            remote(buf.at[b, source], buf.at[b, source], other_sem.at[b, source], sem.at[b, source], ctx=source).wait_recv()

    lanes_bs = bs // 128

    def wide(v):
        return jnp.concatenate([v] * lanes_bs, axis=-1)

    def conv_range(b, j0, nj):
        taps = conv_ref[:, b * bs : (b + 1) * bs].astype(F32)
        pos = wide(seg_b[pl.ds(j0, nj)])
        total = taps[0:1, :] * win[pl.ds(j0 + 3, nj)]
        for k in range(1, 4):
            total = total + taps[k : k + 1, :] * jnp.where(
                pos >= k, win[pl.ds(j0 + 3 - k, nj)], F32(0.0)
            )
        conv[pl.ds(pl.multiple_of(j0 * SUB, SUB * nj), nj * SUB), :] = total.reshape(nj * SUB, bs).astype(BF)

    def gates_range(b, r0, nr):
        grouped = conv[r0 : r0 + nr, :]
        lin_r[r0 : r0 + nr, :] = DOT(grouped, recw[b])
        lin_i[r0 : r0 + nr, :] = DOT(grouped, inpw[b])

    def scan_range(b, j0, nj, carry):
        cum, now = carry
        rows = pl.ds(pl.multiple_of(j0 * SUB, SUB * nj), nj * SUB)
        rate8 = 8.0 * rate_ref[:, b * bs : (b + 1) * bs]
        rate_gate = jax.nn.sigmoid(lin_r[rows, :])
        in_gate = jax.nn.sigmoid(lin_i[rows, :])
        fall = rate_gate * rate8
        starts = wide(seg_b[pl.ds(j0, nj)]).reshape(nj * SUB, bs) == 0
        step = jnp.where(starts, F32(0.0), jnp.exp(-fall))
        scale = jnp.where(starts, F32(1.0), jnp.sqrt(one_minus_exp_minus(2.0 * fall)))
        drive = scale * in_gate * conv[rows, :].astype(F32)
        for j in range(nj):
            a = step[j * SUB : (j + 1) * SUB]
            now = a * now + drive[j * SUB : (j + 1) * SUB]
            cum = a * cum
            decay[b, j0 + j] = cum
            state[b, j0 + j] = now
        return cum, now

    fresh = (jnp.ones((SUB, bs), F32), jnp.zeros((SUB, bs), F32))
    step_j = 8

    def first_pass(b):
        @pl.loop(0, n_ctx)
        def _(source):
            wait_from(recv1, b, r1, s1, source)

        got = recv1[b].reshape(rows_all, bs)
        quarter = rows_all // 4
        for q in range(4):
            block = DOT(perm[q * quarter : (q + 1) * quarter, :], got)
            win[3 + q * quarter // SUB : 3 + (q + 1) * quarter // SUB] = block.reshape(quarter // SUB, SUB, bs)
        tails = [win[seg_rows + k, SUB - 1 : SUB, :] for k in range(3)]
        rim_s[b] = jnp.concatenate(tails + [jnp.zeros((SUB - 3, bs), F32)], axis=0)

        @pl.when(c < n_ctx - 1)
        def _():
            remote(rim_s.at[b], rim_r.at[b], sr.at[b], rr.at[b], ctx=c + 1).start()

        @pl.loop(HEAD // step_j, seg_rows // step_j)
        def _(g):
            conv_range(b, g * step_j, step_j)

        body = rows_all - HEAD * SUB
        half = body // 2 // 16 * 16
        gates_range(b, HEAD * SUB, half)
        gates_range(b, HEAD * SUB + half, body - half)
        cum, now = lax.fori_loop(
            HEAD // step_j,
            seg_rows // step_j,
            lambda g, carry: scan_range(b, g * step_j, step_j, carry),
            fresh,
        )
        ends[b, 2], ends[b, 3] = cum, now

    def second_pass(b):
        @pl.when(c == 0)
        def _():
            rim_r[b] = jnp.zeros((SUB, bs), F32)

        @pl.when(c > 0)
        def _():
            remote(rim_r.at[b], rim_r.at[b], sr.at[b], rr.at[b], ctx=c - 1).wait_recv()

        for k in range(3):
            win[k] = jnp.concatenate(
                [rim_r[b, k : k + 1, :], win[seg_rows + k, 0 : SUB - 1, :]], axis=0
            )
        for g in range(HEAD // step_j):
            conv_range(b, g * step_j, step_j)
        gates_range(b, 0, HEAD * SUB)
        carry = fresh
        for g in range(HEAD // step_j):
            carry = scan_range(b, g * step_j, step_j, carry)
        ends[b, 0], ends[b, 1] = carry
        cum, now = carry[0] * ends[b, 2], ends[b, 2] * carry[1] + ends[b, 3]
        ends[b, 4], ends[b, 5] = cum, now
        whole_c, whole_h = cum[0:1], now[0:1]
        for s in range(1, SUB):
            whole_h = cum[s : s + 1] * whole_h + now[s : s + 1]
            whole_c = cum[s : s + 1] * whole_c
        sum_s[b] = jnp.concatenate([whole_c, whole_h], axis=0)

        @pl.loop(c + 1, n_ctx)
        def _(d):
            remote(sum_s.at[b], sum_r.at[b, c], ss.at[b, d], rs.at[b, c], ctx=d).start()

    def third_pass(b):
        def join(source, incoming):
            remote(sum_r.at[b, source], sum_r.at[b, source], ss.at[b, source], rs.at[b, source], ctx=source).wait_recv()
            both = sum_r[b, source]
            return both[0:1] * incoming + both[1:2]

        incoming = lax.fori_loop(0, c, join, jnp.zeros((1, bs), F32))
        cum, now = ends[b, 4], ends[b, 5]
        lines = [incoming]
        for s in range(SUB - 1):
            lines.append(cum[s : s + 1] * lines[-1] + now[s : s + 1])
        head_in = jnp.concatenate(lines, axis=0)
        body_in = ends[b, 0] * head_in + ends[b, 1]

        def fix(g, into):
            j0 = g * step_j
            full = state[b, pl.ds(j0, step_j)] + decay[b, pl.ds(j0, step_j)] * into
            rows16[pl.ds(pl.multiple_of(j0 * SUB, step_j * SUB), step_j * SUB), :] = full.reshape(step_j * SUB, bs).astype(BF)
            return into

        for g in range(HEAD // step_j):
            fix(g, head_in)
        lax.fori_loop(HEAD // step_j, seg_rows // step_j, fix, body_in)

        @pl.loop(0, ny)
        def _(i):
            k = lax.rem(i + x, ny)
            block = DOT(perm_t[part_rows(k), :], rows16[...]).astype(BF)
            send2[b, pl.ds(lax.rem(y + k, ny) * nz, nz)] = block.reshape(nz, share, bs)
            send_part(send2, recv2, b, k, s2, r2)

    def finish(b):
        @pl.loop(0, ny)
        def _(i):
            other = lax.rem(y + 2 * ny - lax.rem(i + x, ny), ny)

            @pl.loop(0, nz)
            def _(k):
                wait_from(recv2, b, r2, s2, other * nz + k)

            for q in range(per_y):
                owner = other * per_y + q
                shares = mp_rows // share
                rows = pl.ds(pl.multiple_of(owner * mp_rows, mp_rows), mp_rows)
                got = recv2[b, pl.ds(owner * shares, shares)].reshape(mp_rows, bs)
                result = (got.astype(F32) * gate[b, rows, :]).astype(BF)

                @pl.when(owner == m)
                def _():
                    orecv[b, m] = result

                @pl.when(owner != m)
                def _():
                    fin[b, owner] = result
                    remote(fin.at[b, owner], orecv.at[b, m], sm.at[b, owner], rm.at[b, m], mp=owner).start()

    first_pass(0)
    second_pass(0)
    for b in range(1, blocks):
        first_pass(b)
        second_pass(b)
    for b in range(blocks):
        third_pass(b)
    for b in range(1, blocks):

        @pl.loop(0, ny)
        def _(k):
            gate_part(b, k)

    for b in range(blocks):
        finish(b)

    def out_copy(b, source):
        lane = pl.multiple_of(source * (blocks * bs) + b * bs, bs)
        return pltpu.make_async_copy(
            orecv.at[b, source], out_hbm.at[:, pl.ds(lane, bs)], out_sem.at[b, source]
        )

    for b in range(blocks):

        @pl.loop(0, n_mp)
        def _(source):
            @pl.when(source != m)
            def _():
                remote(orecv.at[b, source], orecv.at[b, source], sm.at[b, source], rm.at[b, source], mp=source).wait_recv()

            out_copy(b, source).start()

    for b in range(blocks):

        @pl.loop(0, n_ctx)
        def _(d):
            @pl.when(d != c)
            def _():
                remote(send1.at[b, d], recv1.at[b, c], s1.at[b, d], r1.at[b, c], ctx=d).wait_send()
                remote(send2.at[b, d], recv2.at[b, c], s2.at[b, d], r2.at[b, c], ctx=d).wait_send()

        @pl.loop(c + 1, n_ctx)
        def _(d):
            remote(sum_s.at[b], sum_r.at[b, c], ss.at[b, d], rs.at[b, c], ctx=d).wait_send()

        @pl.when(c < n_ctx - 1)
        def _():
            remote(rim_s.at[b], rim_r.at[b], sr.at[b], rr.at[b], ctx=c + 1).wait_send()

        @pl.loop(0, n_mp)
        def _(d):
            @pl.when(d != m)
            def _():
                remote(fin.at[b, d], orecv.at[b, m], sm.at[b, d], rm.at[b, m], mp=d).wait_send()

            out_copy(b, d).wait()


def body(ny, nz, n_mp, tokens, lru_w, gelu_w, conv_w, recur_w, input_w, rate, seg, src):
    rows_all, depth = tokens.shape
    width = lru_w.shape[1]
    blocks, bs = recur_w.shape[:2]
    n_ctx = ny * nz
    share, seg_rows, mp_rows = rows_all // n_ctx, rows_all // SUB, rows_all // n_mp
    dma = pltpu.SemaphoreType.DMA
    return pl.pallas_call(
        functools.partial(kernel, (ny, nz, n_mp, blocks, bs)),
        out_shape=jax.ShapeDtypeStruct((mp_rows, n_mp * width), BF),
        in_specs=[ANY, ANY, ANY, VMEM, ANY, ANY, VMEM, VMEM, VMEM],
        out_specs=ANY,
        scratch_shapes=[
            pltpu.VMEM((rows_all, depth), BF),
            pltpu.VMEM((blocks, depth, bs), BF),
            pltpu.VMEM((blocks, depth, bs), BF),
            pltpu.VMEM((blocks, bs, bs), BF),
            pltpu.VMEM((blocks, bs, bs), BF),
            pltpu.VMEM((seg_rows, SUB, 128), jnp.int32),
            pltpu.VMEM((seg_rows, SUB, 128), jnp.int32),
            pltpu.VMEM((rows_all, rows_all), BF),
            pltpu.VMEM((rows_all, rows_all), BF),
            pltpu.VMEM((blocks, n_ctx, share, bs), BF),
            pltpu.VMEM((blocks, n_ctx, share, bs), BF),
            pltpu.VMEM((blocks, n_ctx, share, bs), BF),
            pltpu.VMEM((blocks, n_ctx, share, bs), BF),
            pltpu.VMEM((blocks, rows_all, bs), F32),
            pltpu.VMEM((blocks, n_mp, mp_rows, bs), BF),
            pltpu.VMEM((blocks, n_mp, mp_rows, bs), BF),
            pltpu.VMEM((seg_rows + 3, SUB, bs), F32),
            pltpu.VMEM((rows_all, bs), BF),
            pltpu.VMEM((rows_all, bs), F32),
            pltpu.VMEM((rows_all, bs), F32),
            pltpu.VMEM((blocks, seg_rows, SUB, bs), F32),
            pltpu.VMEM((blocks, seg_rows, SUB, bs), F32),
            pltpu.VMEM((blocks, 6, SUB, bs), F32),
            pltpu.VMEM((blocks, SUB, bs), F32),
            pltpu.VMEM((blocks, SUB, bs), F32),
            pltpu.VMEM((blocks, 2, bs), F32),
            pltpu.VMEM((blocks, n_ctx, 2, bs), F32),
            pltpu.VMEM((rows_all, bs), BF),
            dma((ny + 2 * blocks + 2,)),
            dma((blocks, n_mp)),
            dma((blocks, n_ctx)),
            dma((blocks, n_ctx)),
            dma((blocks, n_ctx)),
            dma((blocks, n_ctx)),
            dma((blocks, n_mp)),
            dma((blocks, n_mp)),
            dma((blocks, n_ctx)),
            dma((blocks, n_ctx)),
            dma((blocks,)),
            dma((blocks,)),
        ],
        compiler_params=pltpu.CompilerParams(
            collective_id=0, has_side_effects=True, vmem_limit_bytes=60 * 1024 * 1024
        ),
    )(
        tokens,
        lru_w,
        gelu_w,
        conv_w,
        recur_w,
        input_w,
        rate.reshape(1, width),
        seg.reshape(SUB, seg_rows),
        src.reshape(SUB, seg_rows),
    )


def solution(mesh, ny=None):
    n_ctx, n_mp = mesh.shape["ctx"], mesh.shape["mp"]
    ny = ny or 4
    in_specs = (
        P("ctx", None),
        P(None, "mp"),
        P(None, "mp"),
        P(None, "mp"),
        P("mp", None, None),
        P("mp", None, None),
        P("mp"),
        P("ctx"),
        P("ctx"),
    )
    out_specs = P(("ctx", "mp"), None)
    return jax.shard_map(
        functools.partial(body, ny, n_ctx // ny, n_mp),
        mesh=mesh,
        in_specs=in_specs,
        out_specs=out_specs,
        check_vma=False,
    )
```

time: 249 us -> 80 us (0.32)
  local copies, waits for them, and re-layouts: 80.4 us -> 2.29 us
  Pallas kernels: 0 us -> 77.6 us
  blocking collectives: 52.4 us -> 0 us
  waiting for transfers between devices: 34.4 us -> 0 us
  other arithmetic: 30.2 us -> 0 us
  starting transfers between devices: 25.4 us -> 0 us
  matrix products: 23.9 us -> 0 us
    pallas_call x0 -> x1, Pallas kernels: none -> 77.6 us  [body(): pl.pallas_call(functools.partial(kernel, (ny, nz, n_mp, blocks, bs)), out...]
    all_to_all x2 -> x0, blocking collectives: 52.4 us -> none  [the longest x1 27.1 us: body(): lax.all_to_all(home_out, 'mp', split_axis=0, concat_axis=1, tiled=True)]
    slice x86 -> x0, local copies, waits for them, and re-layouts: 38.6 us -> none  [the longest x68 38.2 us: body(): lax.associative_scan(affine_join, (carried, drive_term), axis=0)]
    all_to_all x2 -> x0, waiting for transfers between devices: 33.9 us -> none  [the longest x1 24.8 us: body(): lax.all_to_all(branch_loader, 'ctx', split_axis=0, concat_axis=0, tiled=T...]
    pad x36 -> x0, local copies, waits for them, and re-layouts: 26.4 us -> none  [body(): lax.associative_scan(affine_join, (carried, drive_term), axis=0)]
    dot_general x4 -> x0, matrix products: 23.9 us -> none  [the longest x1 10.1 us: project_rows(): jnp.dot(rows_in, lru_in_weight, preferred_element_type=jnp.float32)]
    all_to_all x2 -> x0, starting transfers between devices: 19.8 us -> none  [the longest x1 12.2 us: body(): lax.all_to_all(branch_loader, 'ctx', split_axis=0, concat_axis=0, tiled=T...]
    add x38 -> x0, other arithmetic: 13.7 us -> none  [the longest x19 7.75 us: body(): lax.associative_scan(affine_join, (carried, drive_term), axis=0)]
  transfers between devices with their start and end apart: 3 -> 0, of which waited for: 3 -> 0; matrix products, arithmetic and copies ran while one was open for 0% -> 0% of each run, Pallas kernels for 0% -> 0%
where the time goes in v1:
time: 80 us; the launch traced here: 79.9 us
  Pallas kernels  77.6 us (97%)
  local copies, waits for them, and re-layouts  2.29 us (3%)
    pallas_call x1, Pallas kernels, body(): pl.pallas_call(functools.partial(kernel, (ny, nz, n_mp, blocks, bs)), out...  77.6 us
    unnamed x1, local copies, waits for them, and re-layouts  2.29 us

profile of v1, /device:TPU:1, one launch (start us, length us, event | category | flops | bytes accessed | tf_op | source)
XLA Modules:
  0.0 79.9 jit_solution(17361356365597993619)
XLA Ops:
  0.0 77.6 %shard_map.91 = bf16[128,4096]{1,0:T(8,128)(2,1)} custom-call(bf16[1024,4096]{1,0:T(8,128)(2,1)} %tok_hbm.1, bf16[4096,512]{1,0:T(8,128)(2,1)} %lru_hbm.1, bf16[4096,512]{1,0:T(8,128)(2,1)} %gelu_hbm.1, bf16[4,512]{1,0:T(4,128)(2,1)} %conv_ref.1, bf16[2,256,256]{2,1,0:T(8,128)(2,1)} %recur_hbm.1, bf16[2,256,256]{2,1,0:T(8,128)(2,1)} %input_hbm.1, ...), custom_call_target="tpu_custom_call" | custom-call | tf_op jit(solution)/shard_map/pallas_call | solution.py:444
  77.6 2.3 %copy.11 = bf16[128,4096]{1,0:T(8,128)(2,1)} copy(bf16[128,4096]{1,0:T(8,128)(2,1)} %shard_map.91) | data formatting | bytes 2097152

commit v2 on v1

--- a/solution.py
+++ b/solution.py
@@ -14,6 +14,7 @@
 F32 = jnp.float32
 SUB = 8
 HEAD = 16
+WINDOW = 10
 DOT = functools.partial(jnp.dot, preferred_element_type=F32)
 
 
@@ -68,8 +69,10 @@
     out_sem,
     s1,
     r1,
+    w1,
     s2,
     r2,
+    w2,
     sm,
     rm,
     ss,
@@ -79,6 +82,7 @@
 ):
     ny, nz, n_mp, blocks, bs = dims
     n_ctx = ny * nz
+    window = w1.shape[0]
     rows_all, depth = tok.shape
     share = rows_all // n_ctx
     part = rows_all // ny
@@ -140,41 +144,84 @@
     for copy in lru_loads[1:] + gate_loads + gel_loads:
         copy.start()
 
-    src = src_ref[...]
-    idx = (src // rows_all) * share + lax.rem(src, rows_all) - c * share
-    seg = seg_ref[...]
-    for j in range(seg_rows):
-        idx_b[j] = jnp.broadcast_to(idx[:, j : j + 1], (SUB, 128))
-        seg_b[j] = jnp.broadcast_to(seg[:, j : j + 1], (SUB, 128))
-    lanes = lax.broadcasted_iota(jnp.int32, (128, 128), 1)
-
-    @pl.loop(0, rows_all // 128)
-    def _(g):
-        want = idx_b[pl.ds(g * 16, 16)].reshape(128, 128)
-        here = pl.ds(pl.multiple_of(g * 128, 128), 128)
-        for t in range(rows_all // 128):
-            hot = jnp.where(want == lanes + t * 128, F32(1.0), F32(0.0))
-            perm[here, t * 128 : (t + 1) * 128] = hot.astype(BF)
-            perm_t[t * 128 : (t + 1) * 128, here] = hot.T.astype(BF)
-
     def project(b, k):
         rows = part_rows(k)
         branch = DOT(tok[rows, :], lru[b]).astype(BF)
         first = lax.rem(y + k, ny) * nz
         send1[b, pl.ds(first, nz)] = branch.reshape(nz, share, bs)
 
-    def send_part(buf, into, b, k, s_sem, r_sem):
-        first = lax.rem(y + k, ny) * nz
-        for dz in range(nz):
-            d = first + lax.rem(z + dz, nz)
-
-            @pl.when(d != c)
-            def _():
-                remote(buf.at[b, d], into.at[b, c], s_sem.at[b, d], r_sem.at[b, c], ctx=d).start()
-
-            @pl.when(d == c)
-            def _():
-                into[b, c] = buf[b, c]
+    per_group = mp_rows // share
+    group = c // per_group
+    zg = z // per_group
+
+    def target(t, turn):
+        k = lax.rem(t // nz + turn, ny)
+        q, e = lax.rem(t, nz) // per_group, lax.rem(t, per_group)
+        to_y, to_g = lax.rem(y + k, ny), lax.rem(zg + q, per_y)
+        return to_y * nz + to_g * per_group + lax.rem(z + e, per_group)
+
+    def send_one(buf, into, b, t, turn, s_sem, r_sem):
+        d = target(t, turn)
+
+        @pl.when(d != c)
+        def _():
+            remote(buf.at[b, d], into.at[b, c], s_sem, r_sem, ctx=d).start()
+
+        @pl.when(d == c)
+        def _():
+            into[b, c] = buf[b, c]
+
+    def send_part(buf, into, b, i, turn, s_sem, r_sem):
+        for e in range(nz):
+            send_one(buf, into, b, i * nz + e, turn, s_sem, r_sem)
+
+    def window_wait(buf, b, t, turn, slots):
+        d = target(t, turn)
+
+        @pl.when(d != c)
+        def _():
+            remote(buf.at[b, d], buf.at[b, d], slots.at[lax.rem(t, window)], slots.at[lax.rem(t, window)], ctx=d).wait_send()
+
+    def pump(buf, into, b, turn, slots, r_sem):
+        done = [0]
+
+        def more(count):
+            first = done[0]
+            last = min(first + count, n_ctx)
+            done[0] = last
+
+            @pl.loop(first, last)
+            def _(t):
+                @pl.when(t >= window)
+                def _():
+                    window_wait(buf, b, t - window, turn, slots)
+
+                send_one(buf, into, b, t, turn, slots.at[lax.rem(t, window)], r_sem)
+
+        return more
+
+    def window_end(buf, b, turn, slots):
+        @pl.loop(n_ctx - window, n_ctx)
+        def _(t):
+            window_wait(buf, b, t, turn, slots)
+
+    def build_perm():
+        src = src_ref[...]
+        idx = (src // rows_all) * share + lax.rem(src, rows_all) - c * share
+        seg = seg_ref[...]
+        for j in range(seg_rows):
+            idx_b[j] = jnp.broadcast_to(idx[:, j : j + 1], (SUB, 128))
+            seg_b[j] = jnp.broadcast_to(seg[:, j : j + 1], (SUB, 128))
+        lanes = lax.broadcasted_iota(jnp.int32, (128, 128), 1)
+
+        @pl.loop(0, rows_all // 128)
+        def _(g):
+            want = idx_b[pl.ds(g * 16, 16)].reshape(128, 128)
+            here = pl.ds(pl.multiple_of(g * 128, 128), 128)
+            for t in range(rows_all // 128):
+                hot = jnp.where(want == lanes + t * 128, F32(1.0), F32(0.0))
+                perm[here, t * 128 : (t + 1) * 128] = hot.astype(BF)
+                perm_t[t * 128 : (t + 1) * 128, here] = hot.T.astype(BF)
 
     def gate_part(b, k):
         rows = part_rows(k)
@@ -184,23 +231,24 @@
     lru_loads[0].wait()
     load_tok(0).wait()
     project(0, 0)
-    pl.semaphore_wait(barrier, n_ctx + n_mp - 2)
-    send_part(send1, recv1, 0, 0, s1, r1)
+    with jax.named_scope("barrier"):
+        pl.semaphore_wait(barrier, n_ctx + n_mp - 2)
+    send_part(send1, recv1, 0, 0, 0, s1, r1.at[0])
 
     @pl.loop(1, ny)
     def _(k):
         load_tok(k).wait()
         project(0, k)
-        send_part(send1, recv1, 0, k, s1, r1)
-
-    for b in range(1, blocks):
-        lru_loads[b].wait()
-
-        @pl.loop(0, ny)
-        def _(k):
-            project(b, k)
-            send_part(send1, recv1, b, k, s1, r1)
-
+        send_part(send1, recv1, 0, k, 0, s1, r1.at[0])
+
+    lru_loads[1].wait()
+
+    @pl.loop(0, ny)
+    def _(k):
+        project(1, k)
+
+    with jax.named_scope("perm"):
+        build_perm()
     for copy in gate_loads + gel_loads:
         copy.wait()
 
@@ -208,10 +256,11 @@
     def _(k):
         gate_part(0, k)
 
-    def wait_from(buf, b, sem, other_sem, source):
-        @pl.when(source != c)
-        def _():
-            remote(buf.at[b, source], buf.at[b, source], other_sem.at[b, source], sem.at[b, source], ctx=source).wait_recv()
+    def got_all(ref, sem):
+        remote(ref, ref, sem, sem, ctx=lax.rem(c + 1, n_ctx)).wait_recv()
+
+    def sent_all(ref, sem):
+        remote(ref, ref, sem, sem, ctx=lax.rem(c + 1, n_ctx)).wait_send()
 
     lanes_bs = bs // 128
 
@@ -255,16 +304,17 @@
     fresh = (jnp.ones((SUB, bs), F32), jnp.zeros((SUB, bs), F32))
     step_j = 8
 
-    def first_pass(b):
-        @pl.loop(0, n_ctx)
-        def _(source):
-            wait_from(recv1, b, r1, s1, source)
-
+    def first_pass(b, more):
+        with jax.named_scope("wait1"):
+            got_all(recv1.at[b, pl.ds(0, n_ctx - 1)], r1.at[b])
         got = recv1[b].reshape(rows_all, bs)
         quarter = rows_all // 4
-        for q in range(4):
+
+        def permute(q):
             block = DOT(perm[q * quarter : (q + 1) * quarter, :], got)
             win[3 + q * quarter // SUB : 3 + (q + 1) * quarter // SUB] = block.reshape(quarter // SUB, SUB, bs)
+
+        permute(3)
         tails = [win[seg_rows + k, SUB - 1 : SUB, :] for k in range(3)]
         rim_s[b] = jnp.concatenate(tails + [jnp.zeros((SUB - 3, bs), F32)], axis=0)
 
@@ -272,20 +322,29 @@
         def _():
             remote(rim_s.at[b], rim_r.at[b], sr.at[b], rr.at[b], ctx=c + 1).start()
 
+        for q in range(3):
+            more(1)
+            permute(q)
+        more(1)
+
         @pl.loop(HEAD // step_j, seg_rows // step_j)
         def _(g):
             conv_range(b, g * step_j, step_j)
 
         body = rows_all - HEAD * SUB
         half = body // 2 // 16 * 16
+        more(1)
         gates_range(b, HEAD * SUB, half)
         gates_range(b, HEAD * SUB + half, body - half)
-        cum, now = lax.fori_loop(
-            HEAD // step_j,
-            seg_rows // step_j,
-            lambda g, carry: scan_range(b, g * step_j, step_j, carry),
-            fresh,
-        )
+        carry = fresh
+        cuts = (HEAD // step_j, seg_rows // step_j // 2, seg_rows // step_j)
+        for low, high in zip(cuts, cuts[1:]):
+            more(2)
+            carry = lax.fori_loop(
+                low, high, lambda g, was: scan_range(b, g * step_j, step_j, was), carry
+            )
+        cum, now = carry
+        more(2)
         ends[b, 2], ends[b, 3] = cum, now
 
     def second_pass(b):
@@ -295,7 +354,8 @@
 
         @pl.when(c > 0)
         def _():
-            remote(rim_r.at[b], rim_r.at[b], sr.at[b], rr.at[b], ctx=c - 1).wait_recv()
+            with jax.named_scope("waitrim"):
+                got_all(rim_r.at[b], rr.at[b])
 
         for k in range(3):
             win[k] = jnp.concatenate(
@@ -316,17 +376,33 @@
             whole_c = cum[s : s + 1] * whole_c
         sum_s[b] = jnp.concatenate([whole_c, whole_h], axis=0)
 
-        @pl.loop(c + 1, n_ctx)
-        def _(d):
-            remote(sum_s.at[b], sum_r.at[b, c], ss.at[b, d], rs.at[b, c], ctx=d).start()
-
-    def third_pass(b):
+        @pl.loop(y + 1, ny)
+        def _(to_y):
+            for to_z in range(nz):
+                remote(sum_s.at[b], sum_r.at[b, c], ss.at[b, to_y], rs.at[b, y], ctx=to_y * nz + to_z).start()
+
+        @pl.loop(z + 1, nz)
+        def _(to_z):
+            remote(sum_s.at[b], sum_r.at[b, c], ss.at[b, ny + to_z], rs.at[b, ny + z], ctx=y * nz + to_z).start()
+
+    def third_pass(b, send):
         def join(source, incoming):
-            remote(sum_r.at[b, source], sum_r.at[b, source], ss.at[b, source], rs.at[b, source], ctx=source).wait_recv()
             both = sum_r[b, source]
             return both[0:1] * incoming + both[1:2]
 
-        incoming = lax.fori_loop(0, c, join, jnp.zeros((1, bs), F32))
+        def join_row(from_y, incoming):
+            got_all(sum_r.at[b, pl.ds(from_y * nz, nz)], rs.at[b, from_y])
+            for from_z in range(nz):
+                incoming = join(from_y * nz + from_z, incoming)
+            return incoming
+
+        def join_own(from_z, incoming):
+            got_all(sum_r.at[b, y * nz + from_z], rs.at[b, ny + from_z])
+            return join(y * nz + from_z, incoming)
+
+        with jax.named_scope("waitsum"):
+            incoming = lax.fori_loop(0, y, join_row, jnp.zeros((1, bs), F32))
+            incoming = lax.fori_loop(0, z, join_own, incoming)
         cum, now = ends[b, 4], ends[b, 5]
         lines = [incoming]
         for s in range(SUB - 1):
@@ -349,22 +425,26 @@
             k = lax.rem(i + x, ny)
             block = DOT(perm_t[part_rows(k), :], rows16[...]).astype(BF)
             send2[b, pl.ds(lax.rem(y + k, ny) * nz, nz)] = block.reshape(nz, share, bs)
-            send_part(send2, recv2, b, k, s2, r2)
+            if send:
+                send_part(send2, recv2, b, i, x, s2, r2.at[b, group])
 
     def finish(b):
         @pl.loop(0, ny)
         def _(i):
             other = lax.rem(y + 2 * ny - lax.rem(i + x, ny), ny)
-
-            @pl.loop(0, nz)
-            def _(k):
-                wait_from(recv2, b, r2, s2, other * nz + k)
-
             for q in range(per_y):
-                owner = other * per_y + q
-                shares = mp_rows // share
+                owner = other * per_y + lax.rem(zg + per_y - q, per_y)
+
+                @pl.when(owner == group)
+                def _():
+                    got_all(recv2.at[b, pl.ds(0, per_group - 1)], r2.at[b, owner])
+
+                @pl.when(owner != group)
+                def _():
+                    got_all(recv2.at[b, pl.ds(0, per_group)], r2.at[b, owner])
+
                 rows = pl.ds(pl.multiple_of(owner * mp_rows, mp_rows), mp_rows)
-                got = recv2[b, pl.ds(owner * shares, shares)].reshape(mp_rows, bs)
+                got = recv2[b, pl.ds(owner * per_group, per_group)].reshape(mp_rows, bs)
                 result = (got.astype(F32) * gate[b, rows, :]).astype(BF)
 
                 @pl.when(owner == m)
@@ -374,23 +454,41 @@
                 @pl.when(owner != m)
                 def _():
                     fin[b, owner] = result
-                    remote(fin.at[b, owner], orecv.at[b, m], sm.at[b, owner], rm.at[b, m], mp=owner).start()
-
-    first_pass(0)
-    second_pass(0)
-    for b in range(1, blocks):
-        first_pass(b)
-        second_pass(b)
-    for b in range(blocks):
-        third_pass(b)
-    for b in range(1, blocks):
+                    remote(fin.at[b, owner], orecv.at[b, m], sm.at[b], rm.at[b], mp=owner).start()
+
+    scope = jax.named_scope
+    more = pump(send1, recv1, 1, 0, w1, r1.at[1])
+    with scope("sent0"):
+        sent_all(send1.at[0, pl.ds(0, n_ctx - 1)], s1)
+        more(window)
+    with scope("first0"):
+        first_pass(0, more)
+    with scope("second0"):
+        second_pass(0)
+    with scope("more0"):
+        more(n_ctx)
+    with scope("third0"):
+        third_pass(0, False)
+        more = pump(send2, recv2, 0, x, w2, r2.at[0, group])
+        more(window)
+    with scope("first1"):
+        first_pass(1, more)
+    with scope("second1"):
+        second_pass(1)
+    with scope("more1"):
+        more(n_ctx)
+    with scope("third1"):
+        third_pass(1, True)
+
+    with scope("gate1"):
 
         @pl.loop(0, ny)
         def _(k):
-            gate_part(b, k)
+            gate_part(1, k)
 
     for b in range(blocks):
-        finish(b)
+        with scope("finish"):
+            finish(b)
 
     def out_copy(b, source):
         lane = pl.multiple_of(source * (blocks * bs) + b * bs, bs)
@@ -398,40 +496,35 @@
             orecv.at[b, source], out_hbm.at[:, pl.ds(lane, bs)], out_sem.at[b, source]
         )
 
+    with scope("drain"):
+        window_end(send1, 1, 0, w1)
+    window_end(send2, 0, x, w2)
+    sent_all(send2.at[1, pl.ds(0, n_ctx - 1)], s2)
     for b in range(blocks):
 
-        @pl.loop(0, n_mp)
-        def _(source):
-            @pl.when(source != m)
-            def _():
-                remote(orecv.at[b, source], orecv.at[b, source], sm.at[b, source], rm.at[b, source], mp=source).wait_recv()
-
-            out_copy(b, source).start()
-
-    for b in range(blocks):
-
-        @pl.loop(0, n_ctx)
-        def _(d):
-            @pl.when(d != c)
-            def _():
-                remote(send1.at[b, d], recv1.at[b, c], s1.at[b, d], r1.at[b, c], ctx=d).wait_send()
-                remote(send2.at[b, d], recv2.at[b, c], s2.at[b, d], r2.at[b, c], ctx=d).wait_send()
-
-        @pl.loop(c + 1, n_ctx)
-        def _(d):
-            remote(sum_s.at[b], sum_r.at[b, c], ss.at[b, d], rs.at[b, c], ctx=d).wait_send()
+        @pl.loop(y + 1, ny)
+        def _(to_y):
+            sent_all(sum_r.at[b, pl.ds(0, nz)], ss.at[b, to_y])
+
+        @pl.loop(z + 1, nz)
+        def _(to_z):
+            sent_all(sum_s.at[b], ss.at[b, ny + to_z])
 
         @pl.when(c < n_ctx - 1)
         def _():
-            remote(rim_s.at[b], rim_r.at[b], sr.at[b], rr.at[b], ctx=c + 1).wait_send()
-
-        @pl.loop(0, n_mp)
-        def _(d):
-            @pl.when(d != m)
-            def _():
-                remote(fin.at[b, d], orecv.at[b, m], sm.at[b, d], rm.at[b, m], mp=d).wait_send()
-
-            out_copy(b, d).wait()
+            sent_all(rim_s.at[b], sr.at[b])
+
+        sent_all(fin.at[b, pl.ds(0, n_mp - 1)], sm.at[b])
+
+    for b in range(blocks):
+        with jax.named_scope("waitmp"):
+            got_all(orecv.at[b, pl.ds(0, n_mp - 1)], rm.at[b])
+        for source in range(n_mp):
+            out_copy(b, source).start()
+    with jax.named_scope("waitout"):
+        for b in range(blocks):
+            for source in range(n_mp):
+                out_copy(b, source).wait()
 
 
 def body(ny, nz, n_mp, tokens, lru_w, gelu_w, conv_w, recur_w, input_w, rate, seg, src):
@@ -477,14 +570,16 @@
             pltpu.VMEM((rows_all, bs), BF),
             dma((ny + 2 * blocks + 2,)),
             dma((blocks, n_mp)),
-            dma((blocks, n_ctx)),
-            dma((blocks, n_ctx)),
-            dma((blocks, n_ctx)),
-            dma((blocks, n_ctx)),
+            dma,
+            dma((blocks,)),
+            dma((min(WINDOW, n_ctx // 2),)),
+            dma,
             dma((blocks, n_mp)),
-            dma((blocks, n_mp)),
-            dma((blocks, n_ctx)),
-            dma((blocks, n_ctx)),
+            dma((min(WINDOW, n_ctx // 2),)),
+            dma((blocks,)),
+            dma((blocks,)),
+            dma((blocks, ny + nz)),
+            dma((blocks, ny + nz)),
             dma((blocks,)),
             dma((blocks,)),
         ],

time: 80 us -> 73.2 us (0.915)
  Pallas kernels: 77.6 us -> 70.7 us
    pallas_call x1, Pallas kernels: 77.6 us -> 70.7 us  [body(): pl.pallas_call(functools.partial(kernel, (ny, nz, n_mp, blocks, bs)), out...]
where the time goes in v2:
time: 73.2 us; the launch traced here: 73 us
  Pallas kernels  70.7 us (97%)
  local copies, waits for them, and re-layouts  2.29 us (3%)
    pallas_call x1, Pallas kernels, body(): pl.pallas_call(functools.partial(kernel, (ny, nz, n_mp, blocks, bs)), out...  70.7 us
    unnamed x1, local copies, waits for them, and re-layouts  2.29 us

profile of v2, /device:TPU:1, one launch (start us, length us, event | category | flops | bytes accessed | tf_op | source)
XLA Modules:
  0.0 73.0 jit_solution(18315044641706232206)
XLA Ops:
  0.0 70.7 %shard_map.91 = bf16[128,4096]{1,0:T(8,128)(2,1)} custom-call(bf16[1024,4096]{1,0:T(8,128)(2,1)} %tok_hbm.1, bf16[4096,512]{1,0:T(8,128)(2,1)} %lru_hbm.1, bf16[4096,512]{1,0:T(8,128)(2,1)} %gelu_hbm.1, bf16[4,512]{1,0:T(4,128)(2,1)} %conv_ref.1, bf16[2,256,256]{2,1,0:T(8,128)(2,1)} %recur_hbm.1, bf16[2,256,256]{2,1,0:T(8,128)(2,1)} %input_hbm.1, ...), custom_call_target="tpu_custom_call" | custom-call | tf_op jit(solution)/shard_map/pallas_call | solution.py:537
  70.8 2.3 %copy.11 = bf16[128,4096]{1,0:T(8,128)(2,1)} copy(bf16[128,4096]{1,0:T(8,128)(2,1)} %shard_map.91) | data formatting | bytes 2097152

commit v3 on v2

--- a/solution.py
+++ b/solution.py
@@ -14,7 +14,7 @@
 F32 = jnp.float32
 SUB = 8
 HEAD = 16
-WINDOW = 10
+WINDOW = 8
 DOT = functools.partial(jnp.dot, preferred_element_type=F32)
 
 
@@ -92,6 +92,13 @@
     c = lax.axis_index("ctx")
     m = lax.axis_index("mp")
     y, z, x = c // nz, lax.rem(c, nz), m // 2
+
+    def low(v, size):
+        return v & (size - 1)
+
+    def high(v, size):
+        return lax.shift_right_logical(v, size.bit_length() - 1)
+
     barrier = pltpu.get_barrier_semaphore()
 
     @pl.loop(1, n_ctx)
@@ -117,7 +124,7 @@
         )
 
     def part_rows(k):
-        return pl.ds(pl.multiple_of(lax.rem(y + k, ny) * part, part), part)
+        return pl.ds(pl.multiple_of(low(y + k, ny) * part, part), part)
 
     def load_tok(k):
         return pltpu.make_async_copy(
@@ -147,7 +154,7 @@
     def project(b, k):
         rows = part_rows(k)
         branch = DOT(tok[rows, :], lru[b]).astype(BF)
-        first = lax.rem(y + k, ny) * nz
+        first = low(y + k, ny) * nz
         send1[b, pl.ds(first, nz)] = branch.reshape(nz, share, bs)
 
     per_group = mp_rows // share
@@ -155,10 +162,9 @@
     zg = z // per_group
 
     def target(t, turn):
-        k = lax.rem(t // nz + turn, ny)
-        q, e = lax.rem(t, nz) // per_group, lax.rem(t, per_group)
-        to_y, to_g = lax.rem(y + k, ny), lax.rem(zg + q, per_y)
-        return to_y * nz + to_g * per_group + lax.rem(z + e, per_group)
+        to_y = low(y + high(t, nz) + turn, ny)
+        to_g = low(zg + high(t, per_group), per_y)
+        return to_y * nz + to_g * per_group + low(z + t, per_group)
 
     def send_one(buf, into, b, t, turn, s_sem, r_sem):
         d = target(t, turn)
@@ -173,14 +179,14 @@
 
     def send_part(buf, into, b, i, turn, s_sem, r_sem):
         for e in range(nz):
-            send_one(buf, into, b, i * nz + e, turn, s_sem, r_sem)
+            send_one(buf, into, b, jnp.int32(i * nz + e), turn, s_sem, r_sem)
 
     def window_wait(buf, b, t, turn, slots):
         d = target(t, turn)
 
         @pl.when(d != c)
         def _():
-            remote(buf.at[b, d], buf.at[b, d], slots.at[lax.rem(t, window)], slots.at[lax.rem(t, window)], ctx=d).wait_send()
+            remote(buf.at[b, d], buf.at[b, d], slots.at[low(t, window)], slots.at[low(t, window)], ctx=d).wait_send()
 
     def pump(buf, into, b, turn, slots, r_sem):
         done = [0]
@@ -196,7 +202,7 @@
                 def _():
                     window_wait(buf, b, t - window, turn, slots)
 
-                send_one(buf, into, b, t, turn, slots.at[lax.rem(t, window)], r_sem)
+                send_one(buf, into, b, t, turn, slots.at[low(t, window)], r_sem)
 
         return more
 
@@ -422,18 +428,18 @@
 
         @pl.loop(0, ny)
         def _(i):
-            k = lax.rem(i + x, ny)
+            k = low(i + x, ny)
             block = DOT(perm_t[part_rows(k), :], rows16[...]).astype(BF)
-            send2[b, pl.ds(lax.rem(y + k, ny) * nz, nz)] = block.reshape(nz, share, bs)
+            send2[b, pl.ds(low(y + k, ny) * nz, nz)] = block.reshape(nz, share, bs)
             if send:
                 send_part(send2, recv2, b, i, x, s2, r2.at[b, group])
 
-    def finish(b):
-        @pl.loop(0, ny)
+    def finish(b, first, last):
+        @pl.loop(first, last)
         def _(i):
-            other = lax.rem(y + 2 * ny - lax.rem(i + x, ny), ny)
+            other = low(y - i - x, ny)
             for q in range(per_y):
-                owner = other * per_y + lax.rem(zg + per_y - q, per_y)
+                owner = other * per_y + low(zg - q, per_y)
 
                 @pl.when(owner == group)
                 def _():
@@ -461,12 +467,24 @@
     with scope("sent0"):
         sent_all(send1.at[0, pl.ds(0, n_ctx - 1)], s1)
         more(window)
+    with scope("gate1"):
+
+        @pl.loop(0, ny // 2)
+        def _(k):
+            gate_part(1, k)
+
     with scope("first0"):
         first_pass(0, more)
     with scope("second0"):
         second_pass(0)
     with scope("more0"):
         more(n_ctx)
+    with scope("gate1"):
+
+        @pl.loop(ny // 2, ny)
+        def _(k):
+            gate_part(1, k)
+
     with scope("third0"):
         third_pass(0, False)
         more = pump(send2, recv2, 0, x, w2, r2.at[0, group])
@@ -477,18 +495,15 @@
         second_pass(1)
     with scope("more1"):
         more(n_ctx)
+    with scope("early0"):
+        finish(0, 0, ny // 2)
     with scope("third1"):
         third_pass(1, True)
 
-    with scope("gate1"):
-
-        @pl.loop(0, ny)
-        def _(k):
-            gate_part(1, k)
-
-    for b in range(blocks):
-        with scope("finish"):
-            finish(b)
+    with scope("finish0"):
+        finish(0, ny // 2, ny)
+    with scope("finish1"):
+        finish(1, 0, ny)
 
     def out_copy(b, source):
         lane = pl.multiple_of(source * (blocks * bs) + b * bs, bs)
@@ -520,11 +535,8 @@
         with jax.named_scope("waitmp"):
             got_all(orecv.at[b, pl.ds(0, n_mp - 1)], rm.at[b])
         for source in range(n_mp):
-            out_copy(b, source).start()
-    with jax.named_scope("waitout"):
-        for b in range(blocks):
-            for source in range(n_mp):
-                out_copy(b, source).wait()
+            lane = source * (blocks * bs) + b * bs
+            out_hbm[:, lane : lane + bs] = orecv[b, source]
 
 
 def body(ny, nz, n_mp, tokens, lru_w, gelu_w, conv_w, recur_w, input_w, rate, seg, src):
@@ -536,9 +548,9 @@
     dma = pltpu.SemaphoreType.DMA
     return pl.pallas_call(
         functools.partial(kernel, (ny, nz, n_mp, blocks, bs)),
-        out_shape=jax.ShapeDtypeStruct((mp_rows, n_mp * width), BF),
+        out_shape=pltpu.VMEM((mp_rows, n_mp * width), BF),
         in_specs=[ANY, ANY, ANY, VMEM, ANY, ANY, VMEM, VMEM, VMEM],
-        out_specs=ANY,
+        out_specs=VMEM,
         scratch_shapes=[
             pltpu.VMEM((rows_all, depth), BF),
             pltpu.VMEM((blocks, depth, bs), BF),

time: 73.2 us -> 71.6 us (0.978)
  local copies, waits for them, and re-layouts: 2.29 us -> 0.97 us
    unnamed x1, local copies, waits for them, and re-layouts: 2.29 us -> 0.97 us
where the time goes in v3:
time: 71.6 us; the launch traced here: 71.5 us
  Pallas kernels  70.5 us (98%)
  local copies, waits for them, and re-layouts  0.97 us (1%)
    pallas_call x1, Pallas kernels, body(): pl.pallas_call(functools.partial(kernel, (ny, nz, n_mp, blocks, bs)), out...  70.5 us

profile of v3, /device:TPU:1, one launch (start us, length us, event | category | flops | bytes accessed | tf_op | source)
XLA Modules:
  0.0 71.5 jit_solution(7667385287459301355)
XLA Ops:
  0.0 70.5 %shard_map.91 = bf16[128,4096]{1,0:T(8,128)(2,1)S(1)} custom-call(bf16[1024,4096]{1,0:T(8,128)(2,1)} %tok_hbm.1, bf16[4096,512]{1,0:T(8,128)(2,1)} %lru_hbm.1, bf16[4096,512]{1,0:T(8,128)(2,1)} %gelu_hbm.1, bf16[4,512]{1,0:T(4,128)(2,1)} %conv_ref.1, bf16[2,256,256]{2,1,0:T(8,128)(2,1)} %recur_hbm.1, bf16[2,256,256]{2,1,0:T(8,128)(2,1)} %input_hbm.1, ...), custom_call_target="tpu_custom_call" | custom-call | tf_op jit(solution)/shard_map/pallas_call | solution.py:549
  70.5 1.0 %copy.11 = bf16[128,4096]{1,0:T(8,128)(2,1)} copy(bf16[128,4096]{1,0:T(8,128)(2,1)S(1)} %shard_map.91) | data formatting | bytes 2097152

commit v4 on v3

--- a/solution.py
+++ b/solution.py
@@ -14,7 +14,6 @@
 F32 = jnp.float32
 SUB = 8
 HEAD = 16
-WINDOW = 8
 DOT = functools.partial(jnp.dot, preferred_element_type=F32)
 
 
@@ -36,7 +35,7 @@
     rate_ref,
     seg_ref,
     src_ref,
-    out_hbm,
+    out,
     tok,
     lru,
     gel,
@@ -66,13 +65,10 @@
     sum_r,
     rows16,
     load_sem,
-    out_sem,
     s1,
     r1,
-    w1,
     s2,
     r2,
-    w2,
     sm,
     rm,
     ss,
@@ -82,7 +78,7 @@
 ):
     ny, nz, n_mp, blocks, bs = dims
     n_ctx = ny * nz
-    window = w1.shape[0]
+    half, most = n_ctx // 2, n_ctx * 3 // 4
     rows_all, depth = tok.shape
     share = rows_all // n_ctx
     part = rows_all // ny
@@ -101,16 +97,12 @@
 
     barrier = pltpu.get_barrier_semaphore()
 
-    @pl.loop(1, n_ctx)
-    def _(k):
+    for k in sorted(range(1, n_ctx), key=lambda k: -min(k // nz, ny - k // nz) - min(k % nz, nz - k % nz)):
+        peer = low(y + k // nz, ny) * nz + low(z + k % nz, nz)
+        pl.semaphore_signal(barrier, inc=1, device_id={"ctx": peer}, device_id_type=MESH)
+    for k in range(1, n_mp):
         pl.semaphore_signal(
-            barrier, inc=1, device_id={"ctx": lax.rem(c + k, n_ctx)}, device_id_type=MESH
-        )
-
-    @pl.loop(1, n_mp)
-    def _(k):
-        pl.semaphore_signal(
-            barrier, inc=1, device_id={"mp": lax.rem(m + k, n_mp)}, device_id_type=MESH
+            barrier, inc=1, device_id={"mp": low(m + k, n_mp)}, device_id_type=MESH
         )
 
     def remote(src, dst, send_sem, recv_sem, **device):
@@ -181,35 +173,10 @@
         for e in range(nz):
             send_one(buf, into, b, jnp.int32(i * nz + e), turn, s_sem, r_sem)
 
-    def window_wait(buf, b, t, turn, slots):
-        d = target(t, turn)
-
-        @pl.when(d != c)
-        def _():
-            remote(buf.at[b, d], buf.at[b, d], slots.at[low(t, window)], slots.at[low(t, window)], ctx=d).wait_send()
-
-    def pump(buf, into, b, turn, slots, r_sem):
-        done = [0]
-
-        def more(count):
-            first = done[0]
-            last = min(first + count, n_ctx)
-            done[0] = last
-
-            @pl.loop(first, last)
-            def _(t):
-                @pl.when(t >= window)
-                def _():
-                    window_wait(buf, b, t - window, turn, slots)
-
-                send_one(buf, into, b, t, turn, slots.at[low(t, window)], r_sem)
-
-        return more
-
-    def window_end(buf, b, turn, slots):
-        @pl.loop(n_ctx - window, n_ctx)
+    def burst(buf, into, b, first, last, turn, s_sem, r_sem):
+        @pl.loop(first, last)
         def _(t):
-            window_wait(buf, b, t, turn, slots)
+            send_one(buf, into, b, t, turn, s_sem, r_sem)
 
     def build_perm():
         src = src_ref[...]
@@ -239,19 +206,23 @@
     project(0, 0)
     with jax.named_scope("barrier"):
         pl.semaphore_wait(barrier, n_ctx + n_mp - 2)
-    send_part(send1, recv1, 0, 0, 0, s1, r1.at[0])
+    send_part(send1, recv1, 0, 0, 0, s1.at[0], r1.at[0])
 
     @pl.loop(1, ny)
     def _(k):
         load_tok(k).wait()
         project(0, k)
-        send_part(send1, recv1, 0, k, 0, s1, r1.at[0])
+        send_part(send1, recv1, 0, k, 0, s1.at[0], r1.at[0])
 
     lru_loads[1].wait()
 
     @pl.loop(0, ny)
     def _(k):
         project(1, k)
+
+        @pl.when(k < ny // 2)
+        def _():
+            send_part(send1, recv1, 1, k, 0, s1.at[1], r1.at[1])
 
     with jax.named_scope("perm"):
         build_perm()
@@ -276,10 +247,10 @@
     def conv_range(b, j0, nj):
         taps = conv_ref[:, b * bs : (b + 1) * bs].astype(F32)
         pos = wide(seg_b[pl.ds(j0, nj)])
-        total = taps[0:1, :] * win[pl.ds(j0 + 3, nj)]
+        total = taps[0:1, :] * win[b, pl.ds(j0 + 3, nj)]
         for k in range(1, 4):
             total = total + taps[k : k + 1, :] * jnp.where(
-                pos >= k, win[pl.ds(j0 + 3 - k, nj)], F32(0.0)
+                pos >= k, win[b, pl.ds(j0 + 3 - k, nj)], F32(0.0)
             )
         conv[pl.ds(pl.multiple_of(j0 * SUB, SUB * nj), nj * SUB), :] = total.reshape(nj * SUB, bs).astype(BF)
 
@@ -310,47 +281,42 @@
     fresh = (jnp.ones((SUB, bs), F32), jnp.zeros((SUB, bs), F32))
     step_j = 8
 
-    def first_pass(b, more):
+    quarter = rows_all // 4
+
+    def permute(b, q):
+        got = recv1[b].reshape(rows_all, bs)
+        block = DOT(perm[q * quarter : (q + 1) * quarter, :], got)
+        win[b, 3 + q * quarter // SUB : 3 + (q + 1) * quarter // SUB] = block.reshape(quarter // SUB, SUB, bs)
+
+    def arrive(b):
         with jax.named_scope("wait1"):
             got_all(recv1.at[b, pl.ds(0, n_ctx - 1)], r1.at[b])
-        got = recv1[b].reshape(rows_all, bs)
-        quarter = rows_all // 4
-
-        def permute(q):
-            block = DOT(perm[q * quarter : (q + 1) * quarter, :], got)
-            win[3 + q * quarter // SUB : 3 + (q + 1) * quarter // SUB] = block.reshape(quarter // SUB, SUB, bs)
-
-        permute(3)
-        tails = [win[seg_rows + k, SUB - 1 : SUB, :] for k in range(3)]
+        permute(b, 3)
+        tails = [win[b, seg_rows + k, SUB - 1 : SUB, :] for k in range(3)]
         rim_s[b] = jnp.concatenate(tails + [jnp.zeros((SUB - 3, bs), F32)], axis=0)
 
         @pl.when(c < n_ctx - 1)
         def _():
             remote(rim_s.at[b], rim_r.at[b], sr.at[b], rr.at[b], ctx=c + 1).start()
 
+    def first_pass(b):
         for q in range(3):
-            more(1)
-            permute(q)
-        more(1)
+            permute(b, q)
 
         @pl.loop(HEAD // step_j, seg_rows // step_j)
         def _(g):
             conv_range(b, g * step_j, step_j)
 
-        body = rows_all - HEAD * SUB
-        half = body // 2 // 16 * 16
-        more(1)
-        gates_range(b, HEAD * SUB, half)
-        gates_range(b, HEAD * SUB + half, body - half)
-        carry = fresh
-        cuts = (HEAD // step_j, seg_rows // step_j // 2, seg_rows // step_j)
-        for low, high in zip(cuts, cuts[1:]):
-            more(2)
-            carry = lax.fori_loop(
-                low, high, lambda g, was: scan_range(b, g * step_j, step_j, was), carry
-            )
-        cum, now = carry
-        more(2)
+        size = rows_all - HEAD * SUB
+        cut = size // 2 // 16 * 16
+        gates_range(b, HEAD * SUB, cut)
+        gates_range(b, HEAD * SUB + cut, size - cut)
+        cum, now = lax.fori_loop(
+            HEAD // step_j,
+            seg_rows // step_j,
+            lambda g, was: scan_range(b, g * step_j, step_j, was),
+            fresh,
+        )
         ends[b, 2], ends[b, 3] = cum, now
 
     def second_pass(b):
@@ -364,8 +330,8 @@
                 got_all(rim_r.at[b], rr.at[b])
 
         for k in range(3):
-            win[k] = jnp.concatenate(
-                [rim_r[b, k : k + 1, :], win[seg_rows + k, 0 : SUB - 1, :]], axis=0
+            win[b, k] = jnp.concatenate(
+                [rim_r[b, k : k + 1, :], win[b, seg_rows + k, 0 : SUB - 1, :]], axis=0
             )
         for g in range(HEAD // step_j):
             conv_range(b, g * step_j, step_j)
@@ -391,7 +357,7 @@
         def _(to_z):
             remote(sum_s.at[b], sum_r.at[b, c], ss.at[b, ny + to_z], rs.at[b, ny + z], ctx=y * nz + to_z).start()
 
-    def third_pass(b, send):
+    def third_pass(b, sends):
         def join(source, incoming):
             both = sum_r[b, source]
             return both[0:1] * incoming + both[1:2]
@@ -431,8 +397,9 @@
             k = low(i + x, ny)
             block = DOT(perm_t[part_rows(k), :], rows16[...]).astype(BF)
             send2[b, pl.ds(low(y + k, ny) * nz, nz)] = block.reshape(nz, share, bs)
-            if send:
-                send_part(send2, recv2, b, i, x, s2, r2.at[b, group])
+            @pl.when(i < sends)
+            def _():
+                send_part(send2, recv2, b, i, x, s2.at[b], r2.at[b, group])
 
     def finish(b, first, last):
         @pl.loop(first, last)
@@ -463,22 +430,20 @@
                     remote(fin.at[b, owner], orecv.at[b, m], sm.at[b], rm.at[b], mp=owner).start()
 
     scope = jax.named_scope
-    more = pump(send1, recv1, 1, 0, w1, r1.at[1])
-    with scope("sent0"):
-        sent_all(send1.at[0, pl.ds(0, n_ctx - 1)], s1)
-        more(window)
     with scope("gate1"):
 
         @pl.loop(0, ny // 2)
         def _(k):
             gate_part(1, k)
 
+    with scope("arrive0"):
+        arrive(0)
+    burst(send1, recv1, 1, half, most, 0, s1.at[1], r1.at[1])
     with scope("first0"):
-        first_pass(0, more)
+        first_pass(0)
     with scope("second0"):
         second_pass(0)
-    with scope("more0"):
-        more(n_ctx)
+    burst(send1, recv1, 1, most, n_ctx, 0, s1.at[1], r1.at[1])
     with scope("gate1"):
 
         @pl.loop(ny // 2, ny)
@@ -486,35 +451,26 @@
             gate_part(1, k)
 
     with scope("third0"):
-        third_pass(0, False)
-        more = pump(send2, recv2, 0, x, w2, r2.at[0, group])
-        more(window)
+        third_pass(0, ny // 2)
+    with scope("arrive1"):
+        arrive(1)
     with scope("first1"):
-        first_pass(1, more)
+        first_pass(1)
     with scope("second1"):
         second_pass(1)
-    with scope("more1"):
-        more(n_ctx)
+    burst(send2, recv2, 0, half, n_ctx, x, s2.at[0], r2.at[0, group])
     with scope("early0"):
         finish(0, 0, ny // 2)
     with scope("third1"):
-        third_pass(1, True)
-
+        third_pass(1, ny)
     with scope("finish0"):
         finish(0, ny // 2, ny)
     with scope("finish1"):
         finish(1, 0, ny)
 
-    def out_copy(b, source):
-        lane = pl.multiple_of(source * (blocks * bs) + b * bs, bs)
-        return pltpu.make_async_copy(
-            orecv.at[b, source], out_hbm.at[:, pl.ds(lane, bs)], out_sem.at[b, source]
-        )
-
-    with scope("drain"):
-        window_end(send1, 1, 0, w1)
-    window_end(send2, 0, x, w2)
-    sent_all(send2.at[1, pl.ds(0, n_ctx - 1)], s2)
+    for b in range(blocks):
+        sent_all(send1.at[b, pl.ds(0, n_ctx - 1)], s1.at[b])
+        sent_all(send2.at[b, pl.ds(0, n_ctx - 1)], s2.at[b])
     for b in range(blocks):
 
         @pl.loop(y + 1, ny)
@@ -536,7 +492,7 @@
             got_all(orecv.at[b, pl.ds(0, n_mp - 1)], rm.at[b])
         for source in range(n_mp):
             lane = source * (blocks * bs) + b * bs
-            out_hbm[:, lane : lane + bs] = orecv[b, source]
+            out[:, lane : lane + bs] = orecv[b, source]
 
 
 def body(ny, nz, n_mp, tokens, lru_w, gelu_w, conv_w, recur_w, input_w, rate, seg, src):
@@ -568,7 +524,7 @@
             pltpu.VMEM((blocks, rows_all, bs), F32),
             pltpu.VMEM((blocks, n_mp, mp_rows, bs), BF),
             pltpu.VMEM((blocks, n_mp, mp_rows, bs), BF),
-            pltpu.VMEM((seg_rows + 3, SUB, bs), F32),
+            pltpu.VMEM((blocks, seg_rows + 3, SUB, bs), F32),
             pltpu.VMEM((rows_all, bs), BF),
             pltpu.VMEM((rows_all, bs), F32),
             pltpu.VMEM((rows_all, bs), F32),
@@ -581,13 +537,10 @@
             pltpu.VMEM((blocks, n_ctx, 2, bs), F32),
             pltpu.VMEM((rows_all, bs), BF),
             dma((ny + 2 * blocks + 2,)),
+            dma((blocks,)),
+            dma((blocks,)),
+            dma((blocks,)),
             dma((blocks, n_mp)),
-            dma,
-            dma((blocks,)),
-            dma((min(WINDOW, n_ctx // 2),)),
-            dma,
-            dma((blocks, n_mp)),
-            dma((min(WINDOW, n_ctx // 2),)),
             dma((blocks,)),
             dma((blocks,)),
             dma((blocks, ny + nz)),

time: 71.6 us -> 70 us (0.978)
  Pallas kernels: 70.5 us -> 68.8 us
    pallas_call x1, Pallas kernels: 70.5 us -> 68.8 us  [body(): pl.pallas_call(functools.partial(kernel, (ny, nz, n_mp, blocks, bs)), out...]
where the time goes in v4:
time: 70 us; the launch traced here: 69.7 us
  Pallas kernels  68.8 us (98%)
  local copies, waits for them, and re-layouts  0.97 us (1%)
    pallas_call x1, Pallas kernels, body(): pl.pallas_call(functools.partial(kernel, (ny, nz, n_mp, blocks, bs)), out...  68.8 us

profile of v4, /device:TPU:1, one launch (start us, length us, event | category | flops | bytes accessed | tf_op | source)
XLA Modules:
  0.0 69.7 jit_solution(3755539479416024457)
XLA Ops:
  0.0 68.8 %shard_map.91 = bf16[128,4096]{1,0:T(8,128)(2,1)S(1)} custom-call(bf16[1024,4096]{1,0:T(8,128)(2,1)} %tok_hbm.1, bf16[4096,512]{1,0:T(8,128)(2,1)} %lru_hbm.1, bf16[4096,512]{1,0:T(8,128)(2,1)} %gelu_hbm.1, bf16[4,512]{1,0:T(4,128)(2,1)} %conv_ref.1, bf16[2,256,256]{2,1,0:T(8,128)(2,1)} %recur_hbm.1, bf16[2,256,256]{2,1,0:T(8,128)(2,1)} %input_hbm.1, ...), custom_call_target="tpu_custom_call" | custom-call | tf_op jit(solution)/shard_map/pallas_call | solution.py:505
  68.8 1.0 %copy.11 = bf16[128,4096]{1,0:T(8,128)(2,1)} copy(bf16[128,4096]{1,0:T(8,128)(2,1)S(1)} %shard_map.91) | data formatting | bytes 2097152

commit v5 on v4

--- a/solution.py
+++ b/solution.py
@@ -279,7 +279,7 @@
         return cum, now
 
     fresh = (jnp.ones((SUB, bs), F32), jnp.zeros((SUB, bs), F32))
-    step_j = 8
+    step_j = 16
 
     quarter = rows_all // 4
 

time: 70 us -> 69.6 us (level)
  no operation moved by 1% of the time
where the time goes in v5:
time: 69.6 us; the launch traced here: 69.4 us
  Pallas kernels  68.5 us (98%)
  local copies, waits for them, and re-layouts  0.97 us (1%)
    pallas_call x1, Pallas kernels, body(): pl.pallas_call(functools.partial(kernel, (ny, nz, n_mp, blocks, bs)), out...  68.5 us

profile of v5, /device:TPU:1, one launch (start us, length us, event | category | flops | bytes accessed | tf_op | source)
XLA Modules:
  0.0 69.4 jit_solution(4671428524532031058)
XLA Ops:
  0.0 68.5 %shard_map.91 = bf16[128,4096]{1,0:T(8,128)(2,1)S(1)} custom-call(bf16[1024,4096]{1,0:T(8,128)(2,1)} %tok_hbm.1, bf16[4096,512]{1,0:T(8,128)(2,1)} %lru_hbm.1, bf16[4096,512]{1,0:T(8,128)(2,1)} %gelu_hbm.1, bf16[4,512]{1,0:T(4,128)(2,1)} %conv_ref.1, bf16[2,256,256]{2,1,0:T(8,128)(2,1)} %recur_hbm.1, bf16[2,256,256]{2,1,0:T(8,128)(2,1)} %input_hbm.1, ...), custom_call_target="tpu_custom_call" | custom-call | tf_op jit(solution)/shard_map/pallas_call | solution.py:505
  68.5 1.0 %copy.11 = bf16[128,4096]{1,0:T(8,128)(2,1)} copy(bf16[128,4096]{1,0:T(8,128)(2,1)S(1)} %shard_map.91) | data formatting | bytes 2097152
